TPU v7x, 32 devices: a whole 2x2x4 slice. The times are simulated.
32 devices in a mesh: dp: 16 (over z, y, x), tensor: 2 (over core).
Axes of the slice: x: 2, y: 2, z: 4, core: 2. Of those that a mesh axis runs over, the one named last changes fastest.
Arguments:
- layer_in: bfloat16 [32768, 768], P(('dp', 'tensor')), may hold values from -6 to 6
- upstream: bfloat16 [32768, 768], P(('dp', 'tensor')), may hold values from -6 to 6
- lengths: int32 [32], P('dp'), may hold values from 256 to 1024, as said below
- rescale: float32 [768], replicated, may hold values from 0.5 to 1.5
- gating: bfloat16 [768, 1536], P('dp', 'tensor'), may hold values from -0.21875 to 0.21875
- content: bfloat16 [768, 1536], P('dp', 'tensor'), may hold values from -0.21875 to 0.21875
- selector: bfloat16 [768, 128], P('dp'), may hold values from -0.21875 to 0.21875
- timestep: bfloat16 [768, 24], P('dp', 'tensor'), may hold values from -0.21875 to 0.21875
- filters: float32 [4, 1536], P(None, 'tensor'), may hold values from -3 to 3
- kernels: float32 [4, 128], replicated, may hold values from -3 to 3
- biases: float32 [24], P('tensor'), may hold values from -6 to -2
- decays: float32 [24], P('tensor'), may hold values from -1 to 2
- shortcut: float32 [24], P('tensor'), may hold values from 0.5 to 1.5
- amplitude: float32 [1536], P('tensor'), may hold values from 0.5 to 1.5
- outgoing: bfloat16 [1536, 768], P('tensor', 'dp'), may hold values from -0.15625 to 0.15625
Outputs:
- layer_out: bfloat16 [32768, 768], P(('dp', 'tensor'))
- input_grad: bfloat16 [32768, 768], P(('dp', 'tensor'))
- rescale_grad: float32 [768], replicated
- gating_grad: float32 [768, 1536], P('dp', 'tensor')
- content_grad: float32 [768, 1536], P('dp', 'tensor')
- selector_grad: float32 [768, 128], P('dp')
- timestep_grad: float32 [768, 24], P('dp', 'tensor')
- filters_grad: float32 [4, 1536], P(None, 'tensor')
- kernels_grad: float32 [4, 128], replicated
- biases_grad: float32 [24], P('tensor')
- decays_grad: float32 [24], P('tensor')
- shortcut_grad: float32 [24], P('tensor')
- amplitude_grad: float32 [1536], P('tensor')
- outgoing_grad: float32 [1536, 768], P('tensor', 'dp')
Inputs may be any that keep to these rules, and one draw needn't show every extreme that they name: lengths[s] is the number of valid tokens of sequence s; in every draw some sequence fills all 1024 of its slots.
All inputs are finite; a program needn't handle non-finite values.
Results may differ from a plain program's by a relative error of at most 0.011.
Values may be sent and summed in bfloat16 or wider, within the bound.
No kernel may reach another device: no remote copies, remote signals or barrier semaphores. Data moves between devices by JAX's collectives and lax.ppermute only.
A program may use at most 256 MiB of HBM per device.

v0:
```python
import functools
import jax
import jax.numpy as jnp
from jax import lax
from jax.sharding import PartitionSpec as P

INNER_WIDTH = 1536
BLOCK_ROWS = 128
epsilon = 1e-05
precise = lax.Precision.HIGHEST


def causal_conv(values, kernel):
    taps = kernel.shape[0]
    length = values.shape[0]
    padded = jnp.pad(values, ((taps - 1, 0), (0, 0)))
    summed = jnp.zeros_like(values)
    for offset in range(taps):
        summed = summed + padded[offset : offset + length] * kernel[offset]
    return summed


def prepare(mask_full, values_in, select_in, step_in, filters, kernels, biases):
    values_act = jax.nn.silu(causal_conv(values_in, filters)) * mask_full[:, None]
    select_act = jax.nn.silu(causal_conv(select_in, kernels))
    step_sizes = jax.nn.softplus(step_in + biases)
    return (values_act, select_act, step_sizes)


def mix_heads(values_low, select_low, step_sizes, decays, shortcut, gate_in):
    length = values_low.shape[0]
    head_count = step_sizes.shape[1]
    head_width = values_low.shape[1] // head_count
    state_size = select_low.shape[1] // 2
    block_count = length // BLOCK_ROWS
    b_rows = select_low[:, :state_size].reshape(block_count, BLOCK_ROWS, state_size)
    c_rows = select_low[:, state_size:].reshape(block_count, BLOCK_ROWS, state_size)
    head_values = values_low.reshape(block_count, BLOCK_ROWS, head_count, head_width)
    log_decay = (-jnp.exp(decays) * step_sizes).reshape(block_count, BLOCK_ROWS, head_count)
    inclusive = jnp.cumsum(log_decay, axis=1)
    exclusive = inclusive - log_decay
    block_total = inclusive[:, -1]
    inclusive_heads = inclusive.transpose(0, 2, 1)
    exclusive_heads = exclusive.transpose(0, 2, 1)
    places = jnp.arange(BLOCK_ROWS)
    below_mask = (places[:, None] > places[None, :])[None, None, :, :]
    above_mask = (places[:, None] < places[None, :])[None, None, :, :]
    ahead_log = jnp.where(
        below_mask, inclusive_heads[:, :, :, None] - inclusive_heads[:, :, None, :], -1e30
    )
    behind_log = jnp.where(
        above_mask, exclusive_heads[:, :, None, :] - exclusive_heads[:, :, :, None], -1e30
    )
    gram_rows = jnp.einsum("cis,cjs->cij", c_rows, b_rows, precision=precise)
    scaled = head_values * step_sizes.reshape(block_count, BLOCK_ROWS, head_count)[..., None]
    scaled_heads = scaled.transpose(0, 2, 1, 3)
    coupling = gram_rows[:, None, :, :] * (jnp.exp(ahead_log) + jnp.exp(behind_log))
    inner_part = jnp.einsum("chij,chjp->cihp", coupling, scaled_heads, precision=precise)
    decay_out = jnp.exp(block_total[:, None, :] - inclusive)
    decay_in = jnp.exp(exclusive)
    gained_ahead = jnp.einsum("cjh,cjs,cjhp->chsp", decay_out, b_rows, scaled, precision=precise)
    gained_behind = jnp.einsum("cjh,cjs,cjhp->chsp", decay_in, b_rows, scaled, precision=precise)
    carry_decay = jnp.exp(block_total)

    def carry_step(state_now, pieces_in):
        block_decay, gained_state = pieces_in
        return (block_decay[:, None, None] * state_now + gained_state, state_now)

    empty_state = jnp.zeros((head_count, state_size, head_width), jnp.float32)
    _, earlier_state = lax.scan(carry_step, empty_state, (carry_decay, gained_ahead))
    _, later_state = lax.scan(carry_step, empty_state, (carry_decay, gained_behind), reverse=True)
    from_earlier = (
        jnp.einsum("cis,chsp->cihp", c_rows, earlier_state, precision=precise)
        * jnp.exp(inclusive)[..., None]
    )
    from_later = (
        jnp.einsum("cis,chsp->cihp", c_rows, later_state, precision=precise)
        * jnp.exp(block_total[:, None, :] - exclusive)[..., None]
    )
    mixed_out = inner_part + from_earlier + from_later + shortcut[:, None] * head_values
    return mixed_out.reshape(length, head_count * head_width) * jax.nn.silu(gate_in)


def arrange(gathered, tensor_rank, bc_share):
    full_gate, full_values, full_select, full_step, full_out = gathered
    forward_cat = jnp.concatenate((full_gate, full_values, full_select, full_step), axis=1)
    own_select = lax.dynamic_slice_in_dim(full_select, tensor_rank * bc_share, bc_share, 1)
    backward_cat = jnp.concatenate((full_gate, full_values, own_select, full_step), axis=1)
    return (forward_cat, backward_cat, full_out)


def place_slice(piece, tensor_rank, parts):
    last_axis = piece.ndim - 1
    full_shape = piece.shape[:-1] + (piece.shape[-1] * parts,)
    return lax.dynamic_update_slice_in_dim(
        jnp.zeros(full_shape, jnp.float32), piece, tensor_rank * piece.shape[-1], last_axis
    )


def own_slice(summed, tensor_rank, width_own):
    return lax.dynamic_slice_in_dim(summed, tensor_rank * width_own, width_own, summed.ndim - 1)


def on_device(
    layer_in,
    upstream,
    lengths,
    rescale,
    gating,
    content,
    selector,
    timestep,
    filters,
    kernels,
    biases,
    decays,
    shortcut,
    amplitude,
    outgoing,
):
    parts = lax.axis_size("tensor")
    tensor_rank = lax.axis_index("tensor")
    micro_count = lengths.shape[0]
    half_rows = layer_in.shape[0] // micro_count
    length = half_rows * parts
    inner_local = gating.shape[1]
    head_local = timestep.shape[1]
    state_cols = selector.shape[1]
    bc_share = state_cols // parts
    first_only = (tensor_rank == 0).astype(jnp.float32)
    positions = jnp.arange(length)
    own_positions = tensor_rank * half_rows + jnp.arange(half_rows)
    outputs_list = []
    grads_list = []
    total_in = None
    total_out = None
    rescale_acc = jnp.zeros(rescale.shape, jnp.float32)
    filters_acc = jnp.zeros(filters.shape, jnp.float32)
    kernels_acc = jnp.zeros(kernels.shape, jnp.float32)
    biases_acc = jnp.zeros(biases.shape, jnp.float32)
    decays_acc = jnp.zeros(decays.shape, jnp.float32)
    shortcut_acc = jnp.zeros(shortcut.shape, jnp.float32)
    amplitude_acc = jnp.zeros(amplitude.shape, jnp.float32)
    for micro_step in range(micro_count):
        forward_cat, backward_cat, full_out = arrange(
            (
                lax.all_gather(gating, "dp", axis=0, tiled=True),
                lax.all_gather(content, "dp", axis=0, tiled=True),
                lax.all_gather(selector, "dp", axis=0, tiled=True),
                lax.all_gather(timestep, "dp", axis=0, tiled=True),
                lax.all_gather(outgoing, "dp", axis=1, tiled=True),
            ),
            tensor_rank,
            bc_share,
        )
        low_end = micro_step * half_rows
        tok_rows = layer_in[low_end : low_end + half_rows].astype(jnp.float32)
        seq_length = lengths[micro_step]
        mask_own = (own_positions < seq_length).astype(jnp.float32)
        mask_full = (positions < seq_length).astype(jnp.float32)
        inverse = lax.rsqrt(jnp.mean(tok_rows * tok_rows, axis=-1, keepdims=True) + epsilon)
        unit_rows = tok_rows * inverse
        normed = (unit_rows * rescale).astype(jnp.bfloat16)
        sequence = lax.all_gather(normed, "tensor", axis=0, tiled=True)
        projected = jnp.dot(sequence, forward_cat, preferred_element_type=jnp.float32)
        gate_in = projected[:, :inner_local]
        values_in = projected[:, inner_local : 2 * inner_local]
        select_in = projected[:, 2 * inner_local : 2 * inner_local + state_cols]
        step_in = projected[:, 2 * inner_local + state_cols :]
        prepared, prepare_back = jax.vjp(
            functools.partial(prepare, mask_full),
            values_in,
            select_in,
            step_in,
            filters,
            kernels,
            biases,
        )
        values_act, select_act, step_sizes = prepared
        values_low = lax.optimization_barrier(values_act.astype(jnp.bfloat16)).astype(jnp.float32)
        select_low = lax.optimization_barrier(select_act.astype(jnp.bfloat16)).astype(jnp.float32)
        gated_pre, mix_back = jax.vjp(
            mix_heads, values_low, select_low, step_sizes, decays, shortcut, gate_in
        )
        squares = lax.psum(jnp.sum(gated_pre * gated_pre, axis=-1), "tensor")
        out_scale = lax.rsqrt(squares / INNER_WIDTH + epsilon)[:, None]
        gated = (gated_pre * out_scale * amplitude).astype(jnp.bfloat16)
        branch = lax.psum_scatter(
            jnp.dot(gated, full_out, preferred_element_type=jnp.float32).astype(jnp.bfloat16),
            "tensor",
            scatter_dimension=0,
            tiled=True,
        ).astype(jnp.float32)
        outputs_list.append((mask_own[:, None] * (tok_rows + branch)).astype(jnp.bfloat16))
        grad_rows_out = (
            upstream[low_end : low_end + half_rows].astype(jnp.float32) * mask_own[:, None]
        )
        grad_branch = lax.all_gather(
            grad_rows_out.astype(jnp.bfloat16), "tensor", axis=0, tiled=True
        )
        grad_out_mb = jnp.einsum(
            "ri,rd->id", gated, grad_branch, preferred_element_type=jnp.float32
        )
        grad_gated = jnp.einsum(
            "rd,id->ri", grad_branch, full_out, preferred_element_type=jnp.float32
        )
        weighted = grad_gated * amplitude
        cross = lax.psum(jnp.sum(weighted * gated_pre, axis=-1), "tensor")
        grad_pre = out_scale * weighted - gated_pre * out_scale**3 * (cross / INNER_WIDTH)[:, None]
        amplitude_acc = amplitude_acc + jnp.sum(grad_gated * gated_pre * out_scale, axis=0)
        grad_values_low, grad_select_part, grad_steps, grad_decays, grad_shortcut, grad_gate = (
            mix_back(grad_pre)
        )
        grad_select = lax.psum(grad_select_part.astype(jnp.bfloat16), "tensor").astype(jnp.float32)
        grad_values_in, grad_select_in, grad_step_in, grad_filters, grad_kernels, grad_biases = (
            prepare_back((grad_values_low, grad_select, grad_steps))
        )
        grad_proj = jnp.concatenate(
            (grad_gate, grad_values_in, grad_select_in, grad_step_in), axis=1
        ).astype(jnp.bfloat16)
        own_part = lax.dynamic_slice_in_dim(
            grad_proj, 2 * inner_local + tensor_rank * bc_share, bc_share, 1
        )
        grad_back = jnp.concatenate(
            (
                grad_proj[:, : 2 * inner_local],
                own_part,
                grad_proj[:, 2 * inner_local + state_cols :],
            ),
            axis=1,
        )
        grad_in_mb = jnp.einsum(
            "rd,rc->dc", sequence, grad_proj, preferred_element_type=jnp.float32
        )
        grad_normed = lax.psum_scatter(
            jnp.einsum(
                "rc,dc->rd", grad_back, backward_cat, preferred_element_type=jnp.float32
            ).astype(jnp.bfloat16),
            "tensor",
            scatter_dimension=0,
            tiled=True,
        ).astype(jnp.float32)
        weighted_in = grad_normed * rescale
        grad_input = (
            grad_rows_out
            + inverse * weighted_in
            - unit_rows * inverse * jnp.mean(weighted_in * unit_rows, axis=-1, keepdims=True)
        )
        grads_list.append(grad_input.astype(jnp.bfloat16))
        rescale_acc = rescale_acc + jnp.sum(grad_normed * unit_rows, axis=0)
        filters_acc = filters_acc + grad_filters
        kernels_acc = kernels_acc + grad_kernels
        biases_acc = biases_acc + grad_biases
        decays_acc = decays_acc + grad_decays
        shortcut_acc = shortcut_acc + grad_shortcut
        share_in, share_out = (grad_in_mb, grad_out_mb)
        total_in = share_in if total_in is None else total_in + share_in
        total_out = share_out if total_out is None else total_out + share_out
    total_in, total_out = (
        lax.psum_scatter(total_in, "dp", scatter_dimension=0, tiled=True),
        lax.psum_scatter(total_out, "dp", scatter_dimension=1, tiled=True),
    )
    small_sums = lax.psum(
        (
            rescale_acc,
            kernels_acc * first_only,
            place_slice(filters_acc, tensor_rank, parts),
            place_slice(biases_acc, tensor_rank, parts),
            place_slice(decays_acc, tensor_rank, parts),
            place_slice(shortcut_acc, tensor_rank, parts),
            place_slice(amplitude_acc, tensor_rank, parts),
        ),
        ("dp", "tensor"),
    )
    layer_out = jnp.concatenate(outputs_list, axis=0)
    input_grad = jnp.concatenate(grads_list, axis=0)
    gating_grad = total_in[:, :inner_local]
    content_grad = total_in[:, inner_local : 2 * inner_local]
    selector_grad = total_in[:, 2 * inner_local : 2 * inner_local + state_cols]
    timestep_grad = total_in[
        :, 2 * inner_local + state_cols : 2 * inner_local + state_cols + head_local
    ]
    filters_grad = own_slice(small_sums[2], tensor_rank, inner_local)
    biases_grad = own_slice(small_sums[3], tensor_rank, head_local)
    decays_grad = own_slice(small_sums[4], tensor_rank, head_local)
    shortcut_grad = own_slice(small_sums[5], tensor_rank, head_local)
    amplitude_grad = own_slice(small_sums[6], tensor_rank, inner_local)
    return (
        layer_out,
        input_grad,
        small_sums[0],
        gating_grad,
        content_grad,
        selector_grad,
        timestep_grad,
        filters_grad,
        small_sums[1],
        biases_grad,
        decays_grad,
        shortcut_grad,
        amplitude_grad,
        total_out,
    )


def solution(mesh):
    return jax.shard_map(
        on_device,
        mesh=mesh,
        in_specs=(
            P(("dp", "tensor"), None),
            P(("dp", "tensor"), None),
            P("dp"),
            P(),
            P("dp", "tensor"),
            P("dp", "tensor"),
            P("dp", None),
            P("dp", "tensor"),
            P(None, "tensor"),
            P(),
            P("tensor"),
            P("tensor"),
            P("tensor"),
            P("tensor"),
            P("tensor", "dp"),
        ),
        out_specs=(
            P(("dp", "tensor"), None),
            P(("dp", "tensor"), None),
            P(),
            P("dp", "tensor"),
            P("dp", "tensor"),
            P("dp", None),
            P("dp", "tensor"),
            P(None, "tensor"),
            P(),
            P("tensor"),
            P("tensor"),
            P("tensor"),
            P("tensor"),
            P("tensor", "dp"),
        ),
        check_vma=False,
    )
```

profile of v0, /device:TPU:0, one launch (start us, length us, event | category | flops | bytes accessed | tf_op | source)
XLA Modules:
  0.0 1310.7 jit_solution(3207367767485504378)
XLA Ops:
  22.2 42.8 %all-gather = bf16[16,48,12]{1,2,0:T(8,128)(2,1)S(1)} all-gather(bf16[1,48,12]{1,2,0:T(8,128)(2,1)S(1)} %bitcast.647), channel_id=1, replica_groups=mesh['dp'=16,'tensor'=2] {'dp'}, dimensions={0}, use_global_device_ids=true | all-gather | bytes 19584 | tf_op jit(solution)/shard_map/all_gather | solution.py:150
  65.2 36.8 %all_gather.35 = bf16[768,128]{1,0:T(8,128)(2,1)S(1)} all-gather(bf16[48,128]{1,0:T(8,128)(2,1)S(1)} %copy-done.187), channel_id=1, replica_groups=mesh['dp'=16,'tensor'=2] {'dp'}, dimensions={0}, use_global_device_ids=true | all-gather | bytes 208896 | tf_op jit(solution)/shard_map/all_gather | solution.py:149
  104.0 39.9 %all-gather.13.cloned.1.call-done = bf16[768,768]{1,0:T(8,128)(2,1)} async-done(((bf16[48,768]{1,0:T(8,128)(2,1)}), bf16[768,768]{1,0:T(8,128)(2,1)}) %all-gather.13.cloned.1.call-update) | async-done | bytes 1179664 | tf_op jit(solution)/shard_map/all_gather | solution.py:148
  143.8 7.9 fusion.286
  154.5 4.4 fusion.287
  164.4 23.8 %fusion.373 = f32[8,128,12]{2,0,1:T(8,128)S(1)} fusion(f32[8,128,12]{2,0,1:T(8,128)S(1)} %copy.531), kind=kOutput, calls=%fused_computation.612 | output fusion | flops 1560576 | bytes 98304 | tf_op jit(solution)/shard_map/jvp(jit(cumsum))/reduce_window_sum | solution.py:40
  189.6 4.0 slice.208
  211.0 13.0 multiply_convert_fusion.3
  230.2 7.9 fusion.30
  240.2 29.2 %while.138 = (s32[]{:T(128)}, f32[12,64,64]{2,1,0:T(8,128)}, f32[8,12,64,64]{3,2,1,0:T(8,128)}, f32[8,12,1,1]{1,3,2,0:T(1,128)S(1)}, f32[8,12]{1,0:T(8,128)S(1)}...) while((s32[]{:T(128)}, f32[12,64,64]{2,1,0:T(8,128)}, f32[8,12,64,64]{3,2,1,0:T(8,128)}, ...), condition=%wide.region_12.14_spmd.clone, body=%wide.region_11.13_spmd.clone.sunk | while | flops 196611 | bytes 1378044 | solution.py:70
  273.9 8.0 fusion.26
  283.9 29.1 %while.139 = (s32[]{:T(128)}, f32[12,64,64]{2,1,0:T(8,128)}, f32[8,12,64,64]{3,2,1,0:T(8,128)}, f32[8,12,1,1]{1,3,2,0:T(1,128)S(1)}, f32[8,12]{1,0:T(8,128)S(1)}...) while((s32[]{:T(128)}, f32[12,64,64]{2,1,0:T(8,128)}, ...), condition=%wide.region_14.16_spmd.clone, body=%wide.region_13.15_spmd.clone.sunk | while | flops 196612 | bytes 1377556 | solution.py:71
  316.6 5.3 fusion.294
  330.1 16.8 %fusion.97 = f32[8,128,12,64]{1,3,2,0:T(8,128)S(1)} fusion(f32[8,128,12,64]{1,3,2,0:T(8,128)} %bitcast.600, f32[8,128,12,64]{1,3,2,0:T(8,128)} %bitcast.598, f32[8,128,12,64]{1,0,3,2:T(8,128)S(1)} %bitcast.567, f32[8,12,128]{2,1,0:T(8,128)} %copy.535, f32[8,12,128]{2,1,0:T(8,128)} %copy.532, f32[8,128,128]{2,1,0:T(8,128)} %fusion.289, ...), kind=kOutput, calls=%fused_computation.181 | convolution fusion | flops 1222901760 | bytes 13385776 | tf_op jit(solution)/shard_map/jvp(chij,chjp->cihp)/dot_general | solution.py:58
  346.9 3.8 copy.553
  356.1 7.9 fusion.38
  366.2 28.9 %while.136 = (s32[]{:T(128)}, f32[12,64,64]{2,1,0:T(8,128)}, f32[8,12,64,64]{3,2,1,0:T(8,128)}, f32[8,12,1,1]{1,3,2,0:T(1,128)S(1)}, f32[8,12]{1,0:T(8,128)S(1)}...) while((s32[]{:T(128)}, f32[12,64,64]{2,1,0:T(8,128)}, f32[8,12,64,64]{3,2,1,0:T(8,128)}, ...), condition=%wide.region_3.5_spmd.clone, body=%wide.region_2.4_spmd.clone.sunk | while | flops 196611 | bytes 1378044 | solution.py:70
  395.1 3.9 copy.517
  399.9 8.0 fusion.34
  409.9 15.4 %while.137 = (s32[]{:T(128)}, f32[12,64,64]{2,1,0:T(8,128)S(1)}, f32[8,12,64,64]{3,2,1,0:T(8,128)}, f32[8,12,1,1]{1,3,2,0:T(1,128)S(1)}, f32[8,12]{1,0:T(8,128)S...) while((s32[]{:T(128)}, f32[12,64,64]{2,1,0:T(8,128)S(1)}, ...), condition=%wide.region_5.7_spmd.clone, body=%wide.region_4.6_spmd.clone.sunk | while | flops 196612 | bytes 1180948 | solution.py:71
  428.9 5.3 fusion.303
  440.0 16.3 %fusion.101 = f32[8,128,12,64]{1,3,2,0:T(8,128)S(1)} fusion(f32[8,128,12,64]{1,3,2,0:T(8,128)} %bitcast.604, f32[8,128,12,64]{1,3,2,0:T(8,128)} %bitcast.602, f32[8,128,12,64]{1,0,3,2:T(8,128)S(1)} %bitcast.574, f32[8,12,128]{2,1,0:T(8,128)S(1)} %copy.508, f32[8,12,128]{2,1,0:T(8,128)S(1)} %copy.505, f32[8,128,128]{2,1,0:T(8,128)} %fusion.298, ...), kind=kOutput, calls=%fused_computation.186 | convolution fusion | flops 1222901760 | bytes 13385776 | tf_op jit(solution)/shard_map/jvp(chij,chjp->cihp)/dot_general | solution.py:58
  461.8 6.0 multiply_reduce_fusion.19
  470.3 4.9 fusion.376
  475.2 8.3 multiply_reduce_fusion.3
  486.0 13.8 %fusion.64 = (f32[768]{0:T(1024)}, f32[1024,768]{0,1:T(8,128)S(1)}, bf16[1024,768]{0,1:T(8,128)(2,1)}, bf16[1024,768]{0,1:T(8,128)(2,1)}, f32[768]{0:T(1024)}, /*index=5*/f32[1024,768]{0,1:T(8,128)S(1)}) fusion(bf16[1024,768]{0,1:T(8,128)(2,1)} %get-tuple-element.1362, f32[1024,1676]{0,1:T(8,128)} %copy-done.24, f32[1024]{0:T(1024)S(1)} %broadcast_multiply_fusion.19, ...), kind=kLoop, calls=%fused_computation.123 | loop fusion | flops 33028608 | bytes 37782528 | tf_op jit(solution)/shard_map/transpose(jvp())/reduce_sum | solution.py:80
  500.7 3.7 fusion.165
  507.9 10.3 fusion.20
  526.2 10.1 fusion.14
  536.3 4.1 fusion.258
  540.4 12.5 fusion.84
  555.0 51.9 %while.140 = (s32[]{:T(128)}, f32[12,64,64]{2,1,0:T(8,128)}, f32[8,12]{1,0:T(8,128)S(1)}, f32[8,12,64,64]{3,2,1,0:T(8,128)}, f32[8,12,64,64]{2,3,1,0:T(8,128)}, ...) while((s32[]{:T(128)}, f32[12,64,64]{2,1,0:T(8,128)}, ...), condition=%wide.region_22.24_spmd.clone, body=%wide.region_20.23_spmd.clone.sunk | while | flops 294903 | bytes 2556824 | solution.py:71
  606.9 8.2 fusion.32
  615.1 6.2 fusion.89
  621.3 4.2 fusion.264
  627.5 51.8 %while.142 = (s32[]{:T(128)}, f32[12,64,64]{2,1,0:T(8,128)}, f32[8,12]{1,0:T(8,128)S(1)}, f32[8,12,64,64]{3,2,1,0:T(8,128)}, f32[8,12,64,64]{2,3,1,0:T(8,128)}, ...) while((s32[]{:T(128)}, f32[12,64,64]{2,1,0:T(8,128)}, ...), condition=%wide.region_44.46_spmd.clone, body=%wide.region_42.45_spmd.clone.sunk | while | flops 294903 | bytes 2556824 | solution.py:71
  679.3 8.4 fusion.24
  687.8 6.2 fusion.80
  696.0 51.5 %while.141 = (s32[]{:T(128)}, f32[12,64,64]{2,1,0:T(8,128)}, f32[8,12]{1,0:T(8,128)S(1)}, f32[8,12,64,64]{3,2,1,0:T(8,128)}, f32[8,12,64,64]{2,3,1,0:T(8,128)}, ...) while((s32[]{:T(128)}, f32[12,64,64]{2,1,0:T(8,128)}, ...), condition=%wide.region_25.27_spmd.clone, body=%wide.region_23.26_spmd.clone.sunk | while | flops 294904 | bytes 2556336 | solution.py:70
  747.5 12.4 multiply_reduce_fusion.15
  759.9 3.8 copy.564
  765.8 51.8 %while.143 = (s32[]{:T(128)}, f32[12,64,64]{2,1,0:T(8,128)}, f32[8,12]{1,0:T(8,128)S(1)}, f32[8,12,64,64]{3,2,1,0:T(8,128)}, f32[8,12,64,64]{2,3,1,0:T(8,128)}, ...) while((s32[]{:T(128)}, f32[12,64,64]{2,1,0:T(8,128)}, ...), condition=%wide.region_47.49_spmd.clone, body=%wide.region_45.48_spmd.clone.sunk | while | flops 294904 | bytes 2556336 | solution.py:70
  817.6 10.1 fusion.83
  830.6 3.8 copy.596
  838.3 27.9 %fusion.43 = (f32[8,12,128]{2,1,0:T(8,128)}, f32[8,12,128]{2,1,0:T(8,128)}, f32[8,12,128]{2,1,0:T(8,128)}, f32[8,12,128]{2,1,0:T(8,128)}, f32[8,128,128]{2,1,0:T...) fusion(f32[8,12,128]{2,1,0:T(8,128)S(1)} %copy-done.141, ...), kind=kOutput, calls=%fused_computation.89 | convolution fusion | flops 1258717184 | bytes 15351808 | tf_op jit(solution)/shard_map/transpose(jvp(chij,chjp->cihp))/dot_general | solution.py:58
  866.9 5.2 fusion.88
  879.1 5.4 fusion.79
  915.5 6.2 multiply_reduce_fusion.10
  922.0 5.0 multiply_reduce_fusion.6
  927.1 8.5 broadcast_multiply_fusion
  938.1 5.3 concatenate.36
  943.4 8.7 fusion.76
  953.3 4.0 all-reduce.48.cloned.1.call-done
  967.8 4.3 fusion.180
  972.1 6.4 fusion.77
  982.6 4.3 fusion.183
  987.0 4.0 convolution_convert_fusion
  991.1 5.0 convolution_convert_fusion.1
  996.2 5.7 fusion.357
  1002.0 9.4 convolution_add_fusion
  1011.6 4.1 fusion.356
  1023.1 41.6 %all-reduce.42 = (f32[768]{0:T(1024)}, f32[4,1536]{1,0:T(4,128)S(1)}, f32[4,128]{1,0:T(4,128)}, f32[24]{0:T(128)S(1)}, f32[24]{0:T(128)S(1)}, /*index=5*/f32[24]{0:T(128)S(1)}, f32[1536]{0:T(1024)S(1)}) all-reduce(f32[768]{0:T(1024)S(1)} %add.463, ...), channel_id=1, replica_groups=mesh['dp'=16,'tensor'=2] {'dp','tensor'}, use_global_device_ids=true, to_apply=%region_64.66 | all-reduce | flops 9032 | bytes 72256 | tf_op jit(solution)/shard_map/psum | solution.py:263
  1073.4 97.9 %reduce-scatter.15.cloned.1.call-done = f32[48,1676]{1,0:T(8,128)} async-done(((f32[768,1676]{1,0:T(8,128)}), f32[48,1676]{1,0:T(8,128)}) %reduce-scatter.15.cloned.1.call-update) | async-done | bytes 321808 | tf_op jit(solution)/shard_map/reduce_scatter | solution.py:260
  1175.8 128.2 %reduce-scatter.17.cloned.1.call-done = f32[768,48]{0,1:T(8,128)} async-done(((f32[768,768]{0,1:T(8,128)}), f32[768,48]{0,1:T(8,128)}) %reduce-scatter.17.cloned.1.call-update) | async-done | bytes 147472 | tf_op jit(solution)/shard_map/reduce_scatter | solution.py:261
  (1042 shorter events, 514.0 us)
Async XLA Ops:
  7.2 9.6 copy-start.42
  7.2 96.8 %all-gather.17.cloned.1.call-start = ((), (), s32[]{:S(2)}) async-start(), calls=%async_computation.11 | async-start | bytes 2359296 | tf_op jit(solution)/shard_map/all_gather | solution.py:164
  12.7 9.5 copy-start.197
  12.7 52.5 %copy-start.187 = (bf16[48,128]{1,0:T(8,128)(2,1)S(1)}, bf16[48,128]{1,0:T(8,128)(2,1)}, u32[]{:S(2)}) copy-start(bf16[48,128]{1,0:T(8,128)(2,1)} %param.38) | copy-start | bytes 36868
  12.7 91.3 %all-gather.11.cloned.1.call-start = ((), (), s32[]{:S(2)}) async-start(), calls=%async_computation.7 | async-start | bytes 1253376 | tf_op jit(solution)/shard_map/all_gather | solution.py:147
  13.5 88.5 %copy-start.214 = (f32[12]{0:T(128)S(1)}, f32[12]{0:T(128)}, u32[]{:S(2)}) copy-start(f32[12]{0:T(128)} %param.43) | copy-start | bytes 148
  13.5 88.5 %copy-start.188 = (f32[4,768]{1,0:T(4,128)S(1)}, f32[4,768]{1,0:T(4,128)}, u32[]{:S(2)}) copy-start(f32[4,768]{1,0:T(4,128)} %param.40) | copy-start | bytes 36868
  13.5 130.4 %all-gather.13.cloned.1.call-start = ((), (), s32[]{:S(2)}) async-start(), calls=%async_computation.8 | async-start | bytes 1253376 | tf_op jit(solution)/shard_map/all_gather | solution.py:148
  14.2 88.4 %copy-start.207 = (f32[4,128]{1,0:T(4,128)S(1)}, f32[4,128]{1,0:T(4,128)}, u32[]{:S(2)}) copy-start(f32[4,128]{1,0:T(4,128)} %param.41) | copy-start | bytes 6148
  14.2 140.3 %all-gather.9.cloned.1.call-start = ((), (), s32[]{:S(2)}) async-start(), calls=%async_computation.6 | async-start | bytes 2359296 | tf_op jit(solution)/shard_map/all_gather | solution.py:164
  14.8 455.5 %all-gather.21.cloned.1.call-start = ((), (), s32[]{:S(2)}) async-start(), calls=%async_computation.15 | async-start | bytes 2359296 | tf_op jit(solution)/shard_map/all_gather | solution.py:198
  18.3 452.0 %all-gather.15.cloned.1.call-start = ((), (), s32[]{:S(2)}) async-start(), calls=%async_computation.9 | async-start | bytes 1253376 | tf_op jit(solution)/shard_map/all_gather | solution.py:151
  18.9 456.3 %all-gather.19.cloned.1.call-start = ((), (), s32[]{:S(2)}) async-start(), calls=%async_computation.13 | async-start | bytes 2359296 | tf_op jit(solution)/shard_map/all_gather | solution.py:198
  19.6 937.7 %all-reduce.48.cloned.1.call-start = ((), (), s32[]{:S(2)}) async-start(), calls=%async_computation.19 | async-start | bytes 1048576 | tf_op jit(solution)/shard_map/psum | solution.py:214
  65.2 89.4 %copy-start.107 = (bf16[16,48,12]{2,1,0:T(8,128)(2,1)}, bf16[16,48,12]{2,1,0:T(8,128)(2,1)S(1)}, u32[]{:S(2)}) copy-start(bf16[16,48,12]{2,1,0:T(8,128)(2,1)S(1)} %copy.690) | copy-start | bytes 55300
  102.0 56.9 %copy-start.205 = (f32[12]{0:T(128)}, f32[12]{0:T(128)S(1)}, u32[]{:S(2)}) copy-start(f32[12]{0:T(128)S(1)} %exponential_negate_fusion) | copy-start | bytes 148
  102.6 108.4 %copy-start.155 = (f32[768]{0:T(1024)}, f32[768]{0:T(1024)S(1)}, u32[]{:S(2)}) copy-start(f32[768]{0:T(1024)S(1)} %get-tuple-element.1221) | copy-start | bytes 9220
  102.6 108.4 %copy-start.157 = (f32[768]{0:T(1024)}, f32[768]{0:T(1024)S(1)}, u32[]{:S(2)}) copy-start(f32[768]{0:T(1024)S(1)} %get-tuple-element.1222) | copy-start | bytes 9220
  143.8 10.7 copy-start.80
  143.8 10.7 copy-start.81
  151.8 10.0 copy-start.203
  195.8 28.3 %copy-start.15 = (f32[1024,768]{0,1:T(8,128)}, f32[1024,768]{0,1:T(8,128)S(1)}, u32[]{:S(2)}) copy-start(f32[1024,768]{0,1:T(8,128)S(1)} %slice.215) | copy-start | bytes 9437188
  208.2 15.8 %copy-start.133 = (f32[8,12]{0,1:T(8,128)}, f32[8,12]{0,1:T(8,128)S(1)}, u32[]{:S(2)}) copy-start(f32[8,12]{0,1:T(8,128)S(1)} %copy.537) | copy-start | bytes 1156
  225.3 104.7 %copy-start = (f32[96,8,8,128]{3,2,1,0:T(8,128)}, f32[96,8,8,128]{3,2,1,0:T(8,128)S(1)}, u32[]{:S(2)}) copy-start(f32[96,8,8,128]{3,2,1,0:T(8,128)S(1)} %copy.724) | copy-start | bytes 9437188
  353.3 86.7 %copy-start.4 = (f32[96,8,8,128]{3,2,1,0:T(8,128)}, f32[96,8,8,128]{3,2,1,0:T(8,128)S(1)}, u32[]{:S(2)}) copy-start(f32[96,8,8,128]{3,2,1,0:T(8,128)S(1)} %copy.716) | copy-start | bytes 9437188
  437.6 70.3 %copy-start.144 = (f32[8,12,128]{2,1,0:T(8,128)}, f32[8,12,128]{2,1,0:T(8,128)S(1)}, u32[]{:S(2)}) copy-start(f32[8,12,128]{2,1,0:T(8,128)S(1)} %copy.508) | copy-start | bytes 147460
  437.7 63.1 %copy-start.91 = (f32[8,128,12]{1,2,0:T(8,128)}, f32[8,128,12]{1,2,0:T(8,128)S(1)}, u32[]{:S(2)}) copy-start(f32[8,128,12]{1,2,0:T(8,128)S(1)} %copy.519) | copy-start | bytes 147460
  440.0 67.9 %copy-start.140 = (f32[8,12,128]{2,1,0:T(8,128)}, f32[8,12,128]{2,1,0:T(8,128)S(1)}, u32[]{:S(2)}) copy-start(f32[8,12,128]{2,1,0:T(8,128)S(1)} %copy.505) | copy-start | bytes 147460
  440.0 16.3 %copy-start.18 = (f32[8,128,12,64]{1,0,3,2:T(8,128)S(1)}, f32[8,128,12,64]{1,0,3,2:T(8,128)}, u32[]{:S(2)}) copy-start(f32[8,128,12,64]{1,0,3,2:T(8,128)} %copy.553) | copy-start | bytes 9437188
  459.6 26.5 %copy-start.13 = (f32[1024,768]{0,1:T(8,128)}, f32[1024,768]{0,1:T(8,128)S(1)}, u32[]{:S(2)}) copy-start(f32[1024,768]{0,1:T(8,128)S(1)} %get-tuple-element.1369) | copy-start | bytes 9437188
  470.2 15.8 %copy-start.153 = (f32[1024]{0:T(1024)}, f32[1024]{0:T(1024)S(1)}, u32[]{:S(2)}) copy-start(f32[1024]{0:T(1024)S(1)} %get-tuple-element.1440) | copy-start | bytes 12292
  470.2 15.8 %copy-start.136 = (f32[1024]{0:T(1024)}, f32[1024]{0:T(1024)S(1)}, u32[]{:S(2)}) copy-start(f32[1024]{0:T(1024)S(1)} %get-tuple-element.1442) | copy-start | bytes 12292
  500.5 35.8 %copy-start.7 = (f32[96,8,8,128]{3,2,1,0:T(8,128)}, f32[96,8,8,128]{3,2,1,0:T(8,128)S(1)}, u32[]{:S(2)}) copy-start(f32[96,8,8,128]{3,2,1,0:T(8,128)S(1)} %copy.721) | copy-start | bytes 9437188
  526.2 10.1 copy-start.12
  696.0 51.5 %copy-start.202 = (f32[12]{0:T(128)S(1)}, f32[12]{0:T(128)}, u32[]{:S(2)}) copy-start(f32[12]{0:T(128)} %param.44) | copy-start | bytes 148
  747.5 12.4 copy-start.179
  817.6 10.1 copy-start.181
  817.6 10.1 copy-start.34
  817.6 10.1 copy-start.35
  817.6 10.1 copy-start.49
  827.8 10.3 slice-start
  838.2 28.0 %copy-start.79 = (bf16[8,8,8,128]{3,2,1,0:T(8,128)(2,1)S(1)}, bf16[8,8,8,128]{3,2,1,0:T(8,128)(2,1)}, u32[]{:S(2)}) copy-start(bf16[8,8,8,128]{3,2,1,0:T(8,128)(2,1)} %get-tuple-element.1418) | copy-start | bytes 393220
  838.2 28.6 %copy-start.22 = (f32[8,12,64,64]{3,2,1,0:T(8,128)S(1)}, f32[8,12,64,64]{3,2,1,0:T(8,128)}, u32[]{:S(2)}) copy-start(f32[8,12,64,64]{3,2,1,0:T(8,128)} %get-tuple-element.699) | copy-start | bytes 4718596
  838.2 28.6 %copy-start.27 = (f32[8,128,64]{1,2,0:T(8,128)S(1)}, f32[8,128,64]{1,2,0:T(8,128)}, u32[]{:S(2)}) copy-start(f32[8,128,64]{1,2,0:T(8,128)} %copy.511) | copy-start | bytes 786436
  838.3 28.6 %copy-start.36 = (f32[8,12,64,128]{3,2,1,0:T(8,128)S(1)}, f32[8,12,64,128]{3,2,1,0:T(8,128)}, u32[]{:S(2)}) copy-start(f32[8,12,64,128]{3,2,1,0:T(8,128)} %get-tuple-element.1471) | copy-start | bytes 9437188
  872.1 16.5 %copy-start.109 = (f32[8,128,12]{1,2,0:T(8,128)}, f32[8,128,12]{1,2,0:T(8,128)S(1)}, u32[]{:S(2)}) copy-start(f32[8,128,12]{1,2,0:T(8,128)S(1)} %get-tuple-element.1212) | copy-start | bytes 147460
  887.8 11.2 copy-start.100
  887.8 12.7 copy-start.102
  887.8 19.8 %copy-start.96 = (f32[8,128,12]{1,0,2:T(8,128)S(1)}, f32[8,128,12]{1,0,2:T(8,128)}, u32[]{:S(2)}) copy-start(f32[8,128,12]{1,0,2:T(8,128)} %get-tuple-element.1371) | copy-start | bytes 147460
  890.7 24.8 %copy-start.17 = (f32[1024,768]{0,1:T(8,128)S(1)}, f32[1024,768]{0,1:T(8,128)}, u32[]{:S(2)}) copy-start(f32[1024,768]{0,1:T(8,128)} %slice.208) | copy-start | bytes 9437188
  927.1 10.9 copy-start.125
  937.1 82.9 %reduce-scatter.13.cloned.1.call-start = ((), (), s32[]{:S(2)}) async-start(), calls=%async_computation.16 | async-start | bytes 2359296 | tf_op jit(solution)/shard_map/reduce_scatter | solution.py:235
  952.1 11.3 copy-start.190
  952.1 11.3 copy-start.192
  952.1 11.3 copy-start.194
  952.1 11.3 copy-start.196
  972.0 48.0 %reduce-scatter.11.cloned.1.call-start = ((), (), s32[]{:S(2)}) async-start(), calls=%async_computation.14 | async-start | bytes 2359296 | tf_op jit(solution)/shard_map/reduce_scatter | solution.py:235
  986.9 80.9 %reduce-scatter.9.cloned.1.call-start = ((), (), s32[]{:S(2)}) async-start(), calls=%async_computation.12 | async-start | bytes 2359296 | tf_op jit(solution)/shard_map/reduce_scatter | solution.py:188
  991.0 76.8 %reduce-scatter.7.cloned.1.call-start = ((), (), s32[]{:S(2)}) async-start(), calls=%async_computation.10 | async-start | bytes 2359296 | tf_op jit(solution)/shard_map/reduce_scatter | solution.py:188
  996.1 175.2 %reduce-scatter.15.cloned.1.call-start = ((), (), s32[]{:S(2)}) async-start(), calls=%async_computation.17 | async-start | bytes 5849088 | tf_op jit(solution)/shard_map/reduce_scatter | solution.py:260
  1011.4 292.6 %reduce-scatter.17.cloned.1.call-start = ((), (), s32[]{:S(2)}) async-start(), calls=%async_computation.18 | async-start | bytes 2506752 | tf_op jit(solution)/shard_map/reduce_scatter | solution.py:261
  1018.9 48.9 %copy-start.43 = (bf16[1024,768]{1,0:T(8,128)(2,1)S(1)}, bf16[1024,768]{1,0:T(8,128)(2,1)}, u32[]{:S(2)}) copy-start(bf16[1024,768]{1,0:T(8,128)(2,1)} %param.33) | copy-start | bytes 4718596
  1018.9 48.9 %copy-start.168 = (f32[512]{0:T(512)S(1)}, f32[512]{0:T(512)}, u32[]{:S(2)}) copy-start(f32[512]{0:T(512)} %copy-done.167) | copy-start | bytes 6148
  1019.0 48.9 %copy-start.170 = (f32[512]{0:T(512)S(1)}, f32[512]{0:T(512)}, u32[]{:S(2)}) copy-start(f32[512]{0:T(512)} %copy-done.169) | copy-start | bytes 6148
  (169 other events, 721.3 us)
Sparse Core Ops, SparseCore 0:
  12.8 12.4 all-gather.16
  28.1 57.7 all-gather.10
  88.8 55.0 all-gather.12
  145.8 8.6 all-gather.8
  155.9 10.9 all-gather.20
  169.6 57.2 all-gather.14
  228.5 8.6 all-gather.18
  937.2 19.9 all-reduce.47
  972.2 10.2 reduce-scatter.12
  987.0 10.2 reduce-scatter.10
  999.6 10.2 reduce-scatter.8
  1012.0 10.3 reduce-scatter.6
  1028.5 142.8 reduce-scatter.14
  1177.4 126.5 reduce-scatter.16
where the time goes:
time: 1320 us; the launch traced here: 1310 us
  other arithmetic  348 us (26%)
  matrix products  304 us (23%)
  waiting for transfers between devices  276 us (21%)
  local copies, waits for them, and re-layouts  239 us (18%)
  blocking collectives  126 us (10%)
  between operations  16.9 us (1%)
    reduce_scatter x1, waiting for transfers between devices, on_device(): lax.psum_scatter(total_out, 'dp', scatter_dimension=1, tiled=True)  128 us
    reduce_scatter x1, waiting for transfers between devices, on_device(): lax.psum_scatter(total_in, 'dp', scatter_dimension=0, tiled=True)  97.9 us
    dot_general x6, matrix products, mix_heads(): jnp.einsum('chij,chjp->cihp', coupling, scaled_heads, precision=precise)  93.9 us
    dynamic_update_slice x64, other arithmetic, mix_heads(): lax.scan(carry_step, empty_state, (carry_decay, gained_ahead))  71 us
    reduce_sum x32, other arithmetic, carry_step(): return (block_decay[:, None, None] * state_now + gained_state, state_now)  66.1 us
    dynamic_slice x64, local copies, waits for them, and re-layouts, mix_heads(): lax.scan(carry_step, empty_state, (carry_decay, gained_ahead))  62.6 us
    add x32, other arithmetic, carry_step(): return (block_decay[:, None, None] * state_now + gained_state, state_now)  55.8 us
    dot_general x6, matrix products, mix_heads(): jnp.einsum('cjh,cjs,cjhp->chsp', decay_out, b_rows, scaled, precision=pre...  48.9 us
  transfers between devices with their start and end apart: 14, of which 5 were waited for; matrix products, arithmetic and copies ran while one was open for 31% of the time, Pallas kernels for 0%

commit v1 on v0

--- a/solution.py
+++ b/solution.py
@@ -8,6 +8,15 @@
 BLOCK_ROWS = 128
 epsilon = 1e-05
 precise = lax.Precision.HIGHEST
+
+
+def _track_sums_all(page, axis_name, dev_axis):
+    for u in (axis_name, dev_axis):
+        page = lax.psum(page, u)
+    return page
+
+
+recover_paths_up = functools.partial(_track_sums_all, axis_name="dp", dev_axis="tensor")
 
 
 def causal_conv(values, kernel):
@@ -260,7 +269,7 @@
         lax.psum_scatter(total_in, "dp", scatter_dimension=0, tiled=True),
         lax.psum_scatter(total_out, "dp", scatter_dimension=1, tiled=True),
     )
-    small_sums = lax.psum(
+    small_sums = recover_paths_up(
         (
             rescale_acc,
             kernels_acc * first_only,
@@ -269,8 +278,7 @@
             place_slice(decays_acc, tensor_rank, parts),
             place_slice(shortcut_acc, tensor_rank, parts),
             place_slice(amplitude_acc, tensor_rank, parts),
-        ),
-        ("dp", "tensor"),
+        )
     )
     layer_out = jnp.concatenate(outputs_list, axis=0)
     input_grad = jnp.concatenate(grads_list, axis=0)

time: 1320 us -> 1320 us (level)
  blocking collectives: 126 us -> 166 us
  waiting for transfers between devices: 276 us -> 236 us
    reduce_scatter x1, waiting for transfers between devices: 97.9 us -> 57.4 us  [on_device(): lax.psum_scatter(total_in, 'dp', scatter_dimension=0, tiled=True)]
    psum x1 -> x2, blocking collectives: 41.6 us -> 81.9 us  [_track_sums_all(): page = lax.psum(page, u)]
where the time goes in v1:
time: 1320 us; the launch traced here: 1310 us
  other arithmetic  348 us (26%)
  matrix products  304 us (23%)
  local copies, waits for them, and re-layouts  239 us (18%)
  waiting for transfers between devices  236 us (18%)
  blocking collectives  166 us (13%)
  between operations  16.9 us (1%)
    reduce_scatter x1, waiting for transfers between devices, on_device(): lax.psum_scatter(total_out, 'dp', scatter_dimension=1, tiled=True)  128 us
    dot_general x6, matrix products, mix_heads(): jnp.einsum('chij,chjp->cihp', coupling, scaled_heads, precision=precise)  93.9 us
    psum x2, blocking collectives, _track_sums_all(): page = lax.psum(page, u)  81.9 us
    dynamic_update_slice x64, other arithmetic, mix_heads(): lax.scan(carry_step, empty_state, (carry_decay, gained_ahead))  71.2 us
    reduce_sum x32, other arithmetic, carry_step(): return (block_decay[:, None, None] * state_now + gained_state, state_now)  66.2 us
    dynamic_slice x64, local copies, waits for them, and re-layouts, mix_heads(): lax.scan(carry_step, empty_state, (carry_decay, gained_ahead))  62.6 us
    reduce_scatter x1, waiting for transfers between devices, on_device(): lax.psum_scatter(total_in, 'dp', scatter_dimension=0, tiled=True)  57.4 us
    add x32, other arithmetic, carry_step(): return (block_decay[:, None, None] * state_now + gained_state, state_now)  55.9 us
  transfers between devices with their start and end apart: 14, of which 5 were waited for; matrix products, arithmetic and copies ran while one was open for 31% of the time, Pallas kernels for 0%

profile of v1, /device:TPU:0, one launch (start us, length us, event | category | flops | bytes accessed | tf_op | source)
XLA Modules:
  0.0 1310.7 jit_solution(6932351211631521330)
XLA Ops:
  22.2 42.8 %all-gather = bf16[16,48,12]{1,2,0:T(8,128)(2,1)S(1)} all-gather(bf16[1,48,12]{1,2,0:T(8,128)(2,1)S(1)} %bitcast.647), channel_id=1, replica_groups=mesh['dp'=16,'tensor'=2] {'dp'}, dimensions={0}, use_global_device_ids=true | all-gather | bytes 19584 | tf_op jit(solution)/shard_map/all_gather | solution.py:159
  65.2 36.8 %all_gather.35 = bf16[768,128]{1,0:T(8,128)(2,1)S(1)} all-gather(bf16[48,128]{1,0:T(8,128)(2,1)S(1)} %copy-done.187), channel_id=1, replica_groups=mesh['dp'=16,'tensor'=2] {'dp'}, dimensions={0}, use_global_device_ids=true | all-gather | bytes 208896 | tf_op jit(solution)/shard_map/all_gather | solution.py:158
  103.9 39.9 %all-gather.13.cloned.1.call-done = bf16[768,768]{1,0:T(8,128)(2,1)} async-done(((bf16[48,768]{1,0:T(8,128)(2,1)}), bf16[768,768]{1,0:T(8,128)(2,1)}) %all-gather.13.cloned.1.call-update) | async-done | bytes 1179664 | tf_op jit(solution)/shard_map/all_gather | solution.py:157
  143.8 7.9 fusion.286
  154.5 4.4 fusion.287
  164.4 23.8 %fusion.373 = f32[8,128,12]{2,0,1:T(8,128)S(1)} fusion(f32[8,128,12]{2,0,1:T(8,128)S(1)} %copy.531), kind=kOutput, calls=%fused_computation.612 | output fusion | flops 1560576 | bytes 98304 | tf_op jit(solution)/shard_map/jvp(jit(cumsum))/reduce_window_sum | solution.py:49
  189.6 4.0 slice.208
  211.1 13.0 multiply_convert_fusion.3
  230.3 7.9 fusion.30
  240.3 29.2 %while.138 = (s32[]{:T(128)}, f32[12,64,64]{2,1,0:T(8,128)}, f32[8,12,64,64]{3,2,1,0:T(8,128)}, f32[8,12,1,1]{1,3,2,0:T(1,128)S(1)}, f32[8,12]{1,0:T(8,128)S(1)}...) while((s32[]{:T(128)}, f32[12,64,64]{2,1,0:T(8,128)}, f32[8,12,64,64]{3,2,1,0:T(8,128)}, ...), condition=%wide.region_12.14_spmd.clone, body=%wide.region_11.13_spmd.clone.sunk | while | flops 196611 | bytes 1378044 | solution.py:79
  274.0 8.0 fusion.26
  284.1 29.0 %while.139 = (s32[]{:T(128)}, f32[12,64,64]{2,1,0:T(8,128)}, f32[8,12,64,64]{3,2,1,0:T(8,128)}, f32[8,12,1,1]{1,3,2,0:T(1,128)S(1)}, f32[8,12]{1,0:T(8,128)S(1)}...) while((s32[]{:T(128)}, f32[12,64,64]{2,1,0:T(8,128)}, ...), condition=%wide.region_14.16_spmd.clone, body=%wide.region_13.15_spmd.clone.sunk | while | flops 196612 | bytes 1377556 | solution.py:80
  316.5 5.3 fusion.294
  330.0 16.8 %fusion.97 = f32[8,128,12,64]{1,3,2,0:T(8,128)S(1)} fusion(f32[8,128,12,64]{1,3,2,0:T(8,128)} %bitcast.600, f32[8,128,12,64]{1,3,2,0:T(8,128)} %bitcast.598, f32[8,128,12,64]{1,0,3,2:T(8,128)S(1)} %bitcast.567, f32[8,12,128]{2,1,0:T(8,128)} %copy.535, f32[8,12,128]{2,1,0:T(8,128)} %copy.532, f32[8,128,128]{2,1,0:T(8,128)} %fusion.289, ...), kind=kOutput, calls=%fused_computation.181 | convolution fusion | flops 1222901760 | bytes 13385776 | tf_op jit(solution)/shard_map/jvp(chij,chjp->cihp)/dot_general | solution.py:67
  346.8 3.8 copy.553
  356.1 7.9 fusion.38
  366.1 29.1 %while.136 = (s32[]{:T(128)}, f32[12,64,64]{2,1,0:T(8,128)}, f32[8,12,64,64]{3,2,1,0:T(8,128)}, f32[8,12,1,1]{1,3,2,0:T(1,128)S(1)}, f32[8,12]{1,0:T(8,128)S(1)}...) while((s32[]{:T(128)}, f32[12,64,64]{2,1,0:T(8,128)}, f32[8,12,64,64]{3,2,1,0:T(8,128)}, ...), condition=%wide.region_3.5_spmd.clone, body=%wide.region_2.4_spmd.clone.sunk | while | flops 196611 | bytes 1378044 | solution.py:79
  395.2 3.9 copy.517
  400.0 7.9 fusion.34
  410.0 15.5 %while.137 = (s32[]{:T(128)}, f32[12,64,64]{2,1,0:T(8,128)S(1)}, f32[8,12,64,64]{3,2,1,0:T(8,128)}, f32[8,12,1,1]{1,3,2,0:T(1,128)S(1)}, f32[8,12]{1,0:T(8,128)S...) while((s32[]{:T(128)}, f32[12,64,64]{2,1,0:T(8,128)S(1)}, ...), condition=%wide.region_5.7_spmd.clone, body=%wide.region_4.6_spmd.clone.sunk | while | flops 196612 | bytes 1180948 | solution.py:80
  429.1 5.3 fusion.303
  440.2 16.3 %fusion.101 = f32[8,128,12,64]{1,3,2,0:T(8,128)S(1)} fusion(f32[8,128,12,64]{1,3,2,0:T(8,128)} %bitcast.604, f32[8,128,12,64]{1,3,2,0:T(8,128)} %bitcast.602, f32[8,128,12,64]{1,0,3,2:T(8,128)S(1)} %bitcast.574, f32[8,12,128]{2,1,0:T(8,128)S(1)} %copy.508, f32[8,12,128]{2,1,0:T(8,128)S(1)} %copy.505, f32[8,128,128]{2,1,0:T(8,128)} %fusion.298, ...), kind=kOutput, calls=%fused_computation.186 | convolution fusion | flops 1222901760 | bytes 13385776 | tf_op jit(solution)/shard_map/jvp(chij,chjp->cihp)/dot_general | solution.py:67
  462.0 5.9 multiply_reduce_fusion.19
  470.5 4.9 fusion.376
  475.4 8.4 multiply_reduce_fusion.3
  486.2 13.8 %fusion.64 = (f32[768]{0:T(1024)}, f32[1024,768]{0,1:T(8,128)S(1)}, bf16[1024,768]{0,1:T(8,128)(2,1)}, bf16[1024,768]{0,1:T(8,128)(2,1)}, f32[768]{0:T(1024)}, /*index=5*/f32[1024,768]{0,1:T(8,128)S(1)}) fusion(bf16[1024,768]{0,1:T(8,128)(2,1)} %get-tuple-element.1369, f32[1024,1676]{0,1:T(8,128)} %copy-done.24, f32[1024]{0:T(1024)S(1)} %broadcast_multiply_fusion.19, ...), kind=kLoop, calls=%fused_computation.123 | loop fusion | flops 33028608 | bytes 37782528 | tf_op jit(solution)/shard_map/transpose(jvp())/reduce_sum | solution.py:89
  508.1 10.3 fusion.20
  526.4 10.1 fusion.14
  536.6 4.2 fusion.258
  540.7 12.4 fusion.84
  555.2 51.9 %while.140 = (s32[]{:T(128)}, f32[12,64,64]{2,1,0:T(8,128)}, f32[8,12]{1,0:T(8,128)S(1)}, f32[8,12,64,64]{3,2,1,0:T(8,128)}, f32[8,12,64,64]{2,3,1,0:T(8,128)}, ...) while((s32[]{:T(128)}, f32[12,64,64]{2,1,0:T(8,128)}, ...), condition=%wide.region_22.24_spmd.clone, body=%wide.region_20.23_spmd.clone.sunk | while | flops 294903 | bytes 2556824 | solution.py:80
  607.2 8.2 fusion.32
  615.4 6.2 fusion.89
  621.6 4.1 fusion.264
  627.8 51.7 %while.142 = (s32[]{:T(128)}, f32[12,64,64]{2,1,0:T(8,128)}, f32[8,12]{1,0:T(8,128)S(1)}, f32[8,12,64,64]{3,2,1,0:T(8,128)}, f32[8,12,64,64]{2,3,1,0:T(8,128)}, ...) while((s32[]{:T(128)}, f32[12,64,64]{2,1,0:T(8,128)}, ...), condition=%wide.region_44.46_spmd.clone, body=%wide.region_42.45_spmd.clone.sunk | while | flops 294903 | bytes 2556824 | solution.py:80
  679.6 8.4 fusion.24
  688.0 6.2 fusion.80
  696.3 51.7 %while.141 = (s32[]{:T(128)}, f32[12,64,64]{2,1,0:T(8,128)}, f32[8,12]{1,0:T(8,128)S(1)}, f32[8,12,64,64]{3,2,1,0:T(8,128)}, f32[8,12,64,64]{2,3,1,0:T(8,128)}, ...) while((s32[]{:T(128)}, f32[12,64,64]{2,1,0:T(8,128)}, ...), condition=%wide.region_25.27_spmd.clone, body=%wide.region_23.26_spmd.clone.sunk | while | flops 294904 | bytes 2556336 | solution.py:79
  748.0 12.4 multiply_reduce_fusion.15
  760.4 3.8 copy.564
  766.3 51.8 %while.143 = (s32[]{:T(128)}, f32[12,64,64]{2,1,0:T(8,128)}, f32[8,12]{1,0:T(8,128)S(1)}, f32[8,12,64,64]{3,2,1,0:T(8,128)}, f32[8,12,64,64]{2,3,1,0:T(8,128)}, ...) while((s32[]{:T(128)}, f32[12,64,64]{2,1,0:T(8,128)}, ...), condition=%wide.region_47.49_spmd.clone, body=%wide.region_45.48_spmd.clone.sunk | while | flops 294904 | bytes 2556336 | solution.py:79
  818.1 10.1 fusion.83
  831.1 3.8 copy.596
  838.8 27.9 %fusion.43 = (f32[8,12,128]{2,1,0:T(8,128)}, f32[8,12,128]{2,1,0:T(8,128)}, f32[8,12,128]{2,1,0:T(8,128)}, f32[8,12,128]{2,1,0:T(8,128)}, f32[8,128,128]{2,1,0:T...) fusion(f32[8,12,128]{2,1,0:T(8,128)S(1)} %copy-done.141, ...), kind=kOutput, calls=%fused_computation.89 | convolution fusion | flops 1258717184 | bytes 15351808 | tf_op jit(solution)/shard_map/transpose(jvp(chij,chjp->cihp))/dot_general | solution.py:67
  867.4 5.2 fusion.88
  879.6 5.4 fusion.79
  916.0 6.2 multiply_reduce_fusion.10
  922.5 5.0 multiply_reduce_fusion.6
  927.5 8.5 broadcast_multiply_fusion
  938.6 5.2 concatenate.36
  943.9 8.7 fusion.76
  953.8 4.0 all-reduce.49.cloned.1.call-done
  967.7 4.3 fusion.180
  972.1 6.4 fusion.77
  982.6 4.3 fusion.183
  987.0 4.0 convolution_convert_fusion
  991.1 5.0 convolution_convert_fusion.1
  996.2 5.7 fusion.357
  1002.0 9.5 convolution_add_fusion
  1011.7 4.1 fusion.356
  1023.2 77.9 %all-reduce.42 = (f32[768]{0:T(1024)S(1)}, f32[4,1536]{1,0:T(4,128)S(1)}, f32[4,128]{1,0:T(4,128)S(1)}, f32[24]{0:T(128)S(1)}, f32[24]{0:T(128)S(1)}, /*index=5*/f32[24]{0:T(128)S(1)}, f32[1536]{0:T(1024)S(1)}) all-reduce(f32[768]{0:T(1024)S(1)} %add.477, ...), channel_id=1, replica_groups=mesh['dp'=16,'tensor'=2] {'dp'}, use_global_device_ids=true, to_apply=%region_64.66 | all-reduce | flops 9032 | bytes 72256 | tf_op jit(solution)/shard_map/psum | solution.py:15
  1101.1 4.0 all-reduce.43
  1113.8 57.4 %reduce-scatter.15.cloned.1.call-done = f32[48,1676]{1,0:T(8,128)} async-done(((f32[768,1676]{1,0:T(8,128)}), f32[48,1676]{1,0:T(8,128)}) %reduce-scatter.15.cloned.1.call-update) | async-done | bytes 321808 | tf_op jit(solution)/shard_map/reduce_scatter | solution.py:269
  1175.7 128.3 %reduce-scatter.17.cloned.1.call-done = f32[768,48]{0,1:T(8,128)} async-done(((f32[768,768]{0,1:T(8,128)}), f32[768,48]{0,1:T(8,128)}) %reduce-scatter.17.cloned.1.call-update) | async-done | bytes 147472 | tf_op jit(solution)/shard_map/reduce_scatter | solution.py:270
  (1041 shorter events, 517.3 us)
Async XLA Ops:
  7.2 9.6 copy-start.42
  7.2 96.7 %all-gather.17.cloned.1.call-start = ((), (), s32[]{:S(2)}) async-start(), calls=%async_computation.11 | async-start | bytes 2359296 | tf_op jit(solution)/shard_map/all_gather | solution.py:173
  12.6 9.5 copy-start.197
  12.7 52.5 %copy-start.187 = (bf16[48,128]{1,0:T(8,128)(2,1)S(1)}, bf16[48,128]{1,0:T(8,128)(2,1)}, u32[]{:S(2)}) copy-start(bf16[48,128]{1,0:T(8,128)(2,1)} %param.38) | copy-start | bytes 36868
  12.7 91.3 %all-gather.11.cloned.1.call-start = ((), (), s32[]{:S(2)}) async-start(), calls=%async_computation.7 | async-start | bytes 1253376 | tf_op jit(solution)/shard_map/all_gather | solution.py:156
  13.4 88.5 %copy-start.213 = (f32[12]{0:T(128)S(1)}, f32[12]{0:T(128)}, u32[]{:S(2)}) copy-start(f32[12]{0:T(128)} %param.43) | copy-start | bytes 148
  13.4 88.5 %copy-start.188 = (f32[4,768]{1,0:T(4,128)S(1)}, f32[4,768]{1,0:T(4,128)}, u32[]{:S(2)}) copy-start(f32[4,768]{1,0:T(4,128)} %param.40) | copy-start | bytes 36868
  13.5 130.4 %all-gather.13.cloned.1.call-start = ((), (), s32[]{:S(2)}) async-start(), calls=%async_computation.8 | async-start | bytes 1253376 | tf_op jit(solution)/shard_map/all_gather | solution.py:157
  14.2 88.4 %copy-start.207 = (f32[4,128]{1,0:T(4,128)S(1)}, f32[4,128]{1,0:T(4,128)}, u32[]{:S(2)}) copy-start(f32[4,128]{1,0:T(4,128)} %param.41) | copy-start | bytes 6148
  14.2 140.3 %all-gather.9.cloned.1.call-start = ((), (), s32[]{:S(2)}) async-start(), calls=%async_computation.6 | async-start | bytes 2359296 | tf_op jit(solution)/shard_map/all_gather | solution.py:173
  14.8 455.7 %all-gather.21.cloned.1.call-start = ((), (), s32[]{:S(2)}) async-start(), calls=%async_computation.15 | async-start | bytes 2359296 | tf_op jit(solution)/shard_map/all_gather | solution.py:207
  18.2 452.2 %all-gather.15.cloned.1.call-start = ((), (), s32[]{:S(2)}) async-start(), calls=%async_computation.9 | async-start | bytes 1253376 | tf_op jit(solution)/shard_map/all_gather | solution.py:160
  18.8 456.5 %all-gather.19.cloned.1.call-start = ((), (), s32[]{:S(2)}) async-start(), calls=%async_computation.13 | async-start | bytes 2359296 | tf_op jit(solution)/shard_map/all_gather | solution.py:207
  19.6 938.2 %all-reduce.49.cloned.1.call-start = ((), (), s32[]{:S(2)}) async-start(), calls=%async_computation.19 | async-start | bytes 1048576 | tf_op jit(solution)/shard_map/psum | solution.py:223
  65.2 89.4 %copy-start.107 = (bf16[16,48,12]{2,1,0:T(8,128)(2,1)}, bf16[16,48,12]{2,1,0:T(8,128)(2,1)S(1)}, u32[]{:S(2)}) copy-start(bf16[16,48,12]{2,1,0:T(8,128)(2,1)S(1)} %copy.690) | copy-start | bytes 55300
  101.9 56.9 %copy-start.205 = (f32[12]{0:T(128)}, f32[12]{0:T(128)S(1)}, u32[]{:S(2)}) copy-start(f32[12]{0:T(128)S(1)} %exponential_negate_fusion) | copy-start | bytes 148
  102.6 108.5 %copy-start.155 = (f32[768]{0:T(1024)}, f32[768]{0:T(1024)S(1)}, u32[]{:S(2)}) copy-start(f32[768]{0:T(1024)S(1)} %get-tuple-element.1221) | copy-start | bytes 9220
  102.6 108.5 %copy-start.157 = (f32[768]{0:T(1024)}, f32[768]{0:T(1024)S(1)}, u32[]{:S(2)}) copy-start(f32[768]{0:T(1024)S(1)} %get-tuple-element.1222) | copy-start | bytes 9220
  143.8 10.7 copy-start.80
  143.8 10.7 copy-start.81
  151.7 10.0 copy-start.203
  195.8 28.3 %copy-start.15 = (f32[1024,768]{0,1:T(8,128)}, f32[1024,768]{0,1:T(8,128)S(1)}, u32[]{:S(2)}) copy-start(f32[1024,768]{0,1:T(8,128)S(1)} %slice.215) | copy-start | bytes 9437188
  208.3 15.8 %copy-start.133 = (f32[8,12]{0,1:T(8,128)}, f32[8,12]{0,1:T(8,128)S(1)}, u32[]{:S(2)}) copy-start(f32[8,12]{0,1:T(8,128)S(1)} %copy.537) | copy-start | bytes 1156
  225.4 104.7 %copy-start = (f32[96,8,8,128]{3,2,1,0:T(8,128)}, f32[96,8,8,128]{3,2,1,0:T(8,128)S(1)}, u32[]{:S(2)}) copy-start(f32[96,8,8,128]{3,2,1,0:T(8,128)S(1)} %copy.724) | copy-start | bytes 9437188
  353.3 86.8 %copy-start.4 = (f32[96,8,8,128]{3,2,1,0:T(8,128)}, f32[96,8,8,128]{3,2,1,0:T(8,128)S(1)}, u32[]{:S(2)}) copy-start(f32[96,8,8,128]{3,2,1,0:T(8,128)S(1)} %copy.716) | copy-start | bytes 9437188
  437.8 70.3 %copy-start.144 = (f32[8,12,128]{2,1,0:T(8,128)}, f32[8,12,128]{2,1,0:T(8,128)S(1)}, u32[]{:S(2)}) copy-start(f32[8,12,128]{2,1,0:T(8,128)S(1)} %copy.508) | copy-start | bytes 147460
  437.8 63.1 %copy-start.91 = (f32[8,128,12]{1,2,0:T(8,128)}, f32[8,128,12]{1,2,0:T(8,128)S(1)}, u32[]{:S(2)}) copy-start(f32[8,128,12]{1,2,0:T(8,128)S(1)} %copy.519) | copy-start | bytes 147460
  440.2 67.9 %copy-start.140 = (f32[8,12,128]{2,1,0:T(8,128)}, f32[8,12,128]{2,1,0:T(8,128)S(1)}, u32[]{:S(2)}) copy-start(f32[8,12,128]{2,1,0:T(8,128)S(1)} %copy.505) | copy-start | bytes 147460
  440.2 16.3 %copy-start.18 = (f32[8,128,12,64]{1,0,3,2:T(8,128)S(1)}, f32[8,128,12,64]{1,0,3,2:T(8,128)}, u32[]{:S(2)}) copy-start(f32[8,128,12,64]{1,0,3,2:T(8,128)} %copy.553) | copy-start | bytes 9437188
  459.7 26.5 %copy-start.13 = (f32[1024,768]{0,1:T(8,128)}, f32[1024,768]{0,1:T(8,128)S(1)}, u32[]{:S(2)}) copy-start(f32[1024,768]{0,1:T(8,128)S(1)} %get-tuple-element.1376) | copy-start | bytes 9437188
  470.4 15.8 %copy-start.153 = (f32[1024]{0:T(1024)}, f32[1024]{0:T(1024)S(1)}, u32[]{:S(2)}) copy-start(f32[1024]{0:T(1024)S(1)} %get-tuple-element.1447) | copy-start | bytes 12292
  470.4 15.8 %copy-start.136 = (f32[1024]{0:T(1024)}, f32[1024]{0:T(1024)S(1)}, u32[]{:S(2)}) copy-start(f32[1024]{0:T(1024)S(1)} %get-tuple-element.1449) | copy-start | bytes 12292
  500.7 35.8 %copy-start.7 = (f32[96,8,8,128]{3,2,1,0:T(8,128)}, f32[96,8,8,128]{3,2,1,0:T(8,128)S(1)}, u32[]{:S(2)}) copy-start(f32[96,8,8,128]{3,2,1,0:T(8,128)S(1)} %copy.721) | copy-start | bytes 9437188
  526.4 10.2 copy-start.12
  696.3 51.7 %copy-start.202 = (f32[12]{0:T(128)S(1)}, f32[12]{0:T(128)}, u32[]{:S(2)}) copy-start(f32[12]{0:T(128)} %param.44) | copy-start | bytes 148
  748.0 12.4 copy-start.179
  818.1 10.1 copy-start.181
  818.1 10.1 copy-start.34
  818.1 10.1 copy-start.35
  818.1 10.1 copy-start.49
  828.2 10.4 slice-start
  838.7 28.0 %copy-start.79 = (bf16[8,8,8,128]{3,2,1,0:T(8,128)(2,1)S(1)}, bf16[8,8,8,128]{3,2,1,0:T(8,128)(2,1)}, u32[]{:S(2)}) copy-start(bf16[8,8,8,128]{3,2,1,0:T(8,128)(2,1)} %get-tuple-element.1425) | copy-start | bytes 393220
  838.7 28.6 %copy-start.22 = (f32[8,12,64,64]{3,2,1,0:T(8,128)S(1)}, f32[8,12,64,64]{3,2,1,0:T(8,128)}, u32[]{:S(2)}) copy-start(f32[8,12,64,64]{3,2,1,0:T(8,128)} %get-tuple-element.699) | copy-start | bytes 4718596
  838.7 28.6 %copy-start.27 = (f32[8,128,64]{1,2,0:T(8,128)S(1)}, f32[8,128,64]{1,2,0:T(8,128)}, u32[]{:S(2)}) copy-start(f32[8,128,64]{1,2,0:T(8,128)} %copy.511) | copy-start | bytes 786436
  838.7 28.6 %copy-start.36 = (f32[8,12,64,128]{3,2,1,0:T(8,128)S(1)}, f32[8,12,64,128]{3,2,1,0:T(8,128)}, u32[]{:S(2)}) copy-start(f32[8,12,64,128]{3,2,1,0:T(8,128)} %get-tuple-element.1478) | copy-start | bytes 9437188
  872.6 16.5 %copy-start.109 = (f32[8,128,12]{1,2,0:T(8,128)}, f32[8,128,12]{1,2,0:T(8,128)S(1)}, u32[]{:S(2)}) copy-start(f32[8,128,12]{1,2,0:T(8,128)S(1)} %get-tuple-element.1212) | copy-start | bytes 147460
  888.3 11.2 copy-start.100
  888.3 12.7 copy-start.102
  888.3 19.8 %copy-start.96 = (f32[8,128,12]{1,0,2:T(8,128)S(1)}, f32[8,128,12]{1,0,2:T(8,128)}, u32[]{:S(2)}) copy-start(f32[8,128,12]{1,0,2:T(8,128)} %get-tuple-element.1378) | copy-start | bytes 147460
  891.2 24.7 %copy-start.17 = (f32[1024,768]{0,1:T(8,128)S(1)}, f32[1024,768]{0,1:T(8,128)}, u32[]{:S(2)}) copy-start(f32[1024,768]{0,1:T(8,128)} %slice.208) | copy-start | bytes 9437188
  927.5 11.0 copy-start.125
  937.6 82.5 %reduce-scatter.13.cloned.1.call-start = ((), (), s32[]{:S(2)}) async-start(), calls=%async_computation.16 | async-start | bytes 2359296 | tf_op jit(solution)/shard_map/reduce_scatter | solution.py:244
  952.6 10.8 copy-start.190
  952.6 10.8 copy-start.192
  952.6 10.8 copy-start.194
  952.6 10.8 copy-start.196
  972.0 48.1 %reduce-scatter.11.cloned.1.call-start = ((), (), s32[]{:S(2)}) async-start(), calls=%async_computation.14 | async-start | bytes 2359296 | tf_op jit(solution)/shard_map/reduce_scatter | solution.py:244
  986.9 121.3 %reduce-scatter.9.cloned.1.call-start = ((), (), s32[]{:S(2)}) async-start(), calls=%async_computation.12 | async-start | bytes 2359296 | tf_op jit(solution)/shard_map/reduce_scatter | solution.py:197
  991.0 117.2 %reduce-scatter.7.cloned.1.call-start = ((), (), s32[]{:S(2)}) async-start(), calls=%async_computation.10 | async-start | bytes 2359296 | tf_op jit(solution)/shard_map/reduce_scatter | solution.py:197
  996.1 175.1 %reduce-scatter.15.cloned.1.call-start = ((), (), s32[]{:S(2)}) async-start(), calls=%async_computation.17 | async-start | bytes 5849088 | tf_op jit(solution)/shard_map/reduce_scatter | solution.py:269
  1011.5 292.5 %reduce-scatter.17.cloned.1.call-start = ((), (), s32[]{:S(2)}) async-start(), calls=%async_computation.18 | async-start | bytes 2506752 | tf_op jit(solution)/shard_map/reduce_scatter | solution.py:270
  1019.0 89.2 %copy-start.43 = (bf16[1024,768]{1,0:T(8,128)(2,1)S(1)}, bf16[1024,768]{1,0:T(8,128)(2,1)}, u32[]{:S(2)}) copy-start(bf16[1024,768]{1,0:T(8,128)(2,1)} %param.33) | copy-start | bytes 4718596
  1019.0 89.2 %copy-start.168 = (f32[512]{0:T(512)S(1)}, f32[512]{0:T(512)}, u32[]{:S(2)}) copy-start(f32[512]{0:T(512)} %copy-done.167) | copy-start | bytes 6148
  1019.0 89.2 %copy-start.170 = (f32[512]{0:T(512)S(1)}, f32[512]{0:T(512)}, u32[]{:S(2)}) copy-start(f32[512]{0:T(512)} %copy-done.169) | copy-start | bytes 6148
  (168 other events, 717.3 us)
Sparse Core Ops, SparseCore 0:
  12.8 12.4 all-gather.16
  28.1 57.7 all-gather.10
  88.8 55.0 all-gather.12
  145.8 8.6 all-gather.8
  155.9 10.9 all-gather.20
  169.6 57.2 all-gather.14
  228.4 8.6 all-gather.18
  937.7 19.9 all-reduce.48
  972.1 10.2 reduce-scatter.12
  987.0 10.2 reduce-scatter.10
  999.6 10.2 reduce-scatter.8
  1012.0 10.2 reduce-scatter.6
  1028.4 142.7 reduce-scatter.14
  1177.3 126.5 reduce-scatter.16
